TPU v7x, 256 devices: a whole 4x4x8 slice. The times are simulated.
256 devices in a mesh: section: 8 (over x, z_lo), mp: 32 (over y, z_hi, core).
Axes of the slice: x: 4, y: 4, z: 8 (z_hi: 4, z_lo: 2; z = z_hi * 2 + z_lo), core: 2. Of those that a mesh axis runs over, the one named last changes fastest.
Arguments:
- enc_final: bfloat16 [8, 128, 4096], P('section', None, 'mp'), may hold values from -64 to 64
- enc_len: int32 [8], replicated, may hold values from 32 to 128, as said below
- kv_weight: bfloat16 [8, 4096, 2, 4096], P('section', None, None, 'mp'), may hold values from -1 to 1
- queries: bfloat16 [8, 8, 512, 4096], P('section', None, None, 'mp'), may hold values from -4096 to 4096
- d_context: bfloat16 [8, 8, 512, 4096], P('section', None, None, 'mp'), may hold values from -6 to 6
Outputs:
- context: bfloat16 [8, 8, 512, 4096], P('section', None, None, 'mp')
- query_grad: bfloat16 [8, 8, 512, 4096], P('section', None, None, 'mp')
- kv_weight_grad: bfloat16 [8, 4096, 2, 4096], P('section', None, None, 'mp')
- enc_grad: bfloat16 [8, 128, 4096], P('section', None, 'mp')
Inputs may be any that keep to these rules, and one draw needn't show every extreme that they name: `enc_len`: some microbatch has exactly 128 valid positions.
All inputs are finite; a program needn't handle non-finite values.
Results may differ from a plain program's by a relative error of at most 0.02.
Values may be sent and summed in bfloat16 or wider, within the bound.
No kernel may reach another device: no remote copies, remote signals or barrier semaphores. Data moves between devices by JAX's collectives and lax.ppermute only.
A program may use at most 128 MiB of HBM per device.

v0:
```python
import jax
import jax.numpy as jnp
from jax import lax
from jax.sharding import PartitionSpec as P

HD = 64


def shards(enc_final, enc_len, kv_weight, queries, d_context):
    model_width = kv_weight.shape[1]
    local_cols = kv_weight.shape[3]
    heads_dev = local_cols // HD
    micro = queries.shape[1]
    targets = queries.shape[2]
    sources = enc_final.shape[1]
    across = lax.all_gather(enc_final, "section", axis=0, tiled=True)
    states = lax.all_gather(across, "mp", axis=2, tiled=True)
    states_flat = states.reshape(micro * sources, model_width)
    weight_flat = kv_weight.reshape(model_width, 2 * local_cols)
    key_value = jnp.dot(states_flat, weight_flat, preferred_element_type=jnp.float32).astype(
        jnp.bfloat16
    )
    key_value = key_value.reshape(micro, sources, 2, heads_dev, HD)
    key_heads = key_value[:, :, 0]
    value_heads = key_value[:, :, 1]
    query_heads = queries.reshape(micro, targets, heads_dev, HD)
    grad_heads = d_context.reshape(micro, targets, heads_dev, HD)
    factor = HD ** (-0.5)
    scores = (
        jnp.einsum("mthd,mshd->mhts", query_heads, key_heads, preferred_element_type=jnp.float32)
        * factor
    )
    position = jnp.arange(sources, dtype=jnp.int32)
    valid_key = position[None, :] < enc_len[:, None]
    scores = jnp.where(valid_key[:, None, None, :], scores, -1e30)
    row_peak = jnp.max(scores, axis=-1, keepdims=True)
    exponent = jnp.exp(scores - row_peak)
    attn_prob = exponent / jnp.sum(exponent, axis=-1, keepdims=True)
    rounded = attn_prob.astype(jnp.bfloat16)
    context = jnp.einsum(
        "mhts,mshd->mthd", rounded, value_heads, preferred_element_type=jnp.float32
    ).astype(jnp.bfloat16)
    value_grad = jnp.einsum(
        "mhts,mthd->mshd", rounded, grad_heads, preferred_element_type=jnp.float32
    )
    prob_grad = jnp.einsum(
        "mthd,mshd->mhts", grad_heads, value_heads, preferred_element_type=jnp.float32
    )
    score_grad = attn_prob * (prob_grad - jnp.sum(prob_grad * attn_prob, axis=-1, keepdims=True))
    score_rounded = (score_grad * factor).astype(jnp.bfloat16)
    key_grad = jnp.einsum(
        "mhts,mthd->mshd", score_rounded, query_heads, preferred_element_type=jnp.float32
    )
    query_grad = jnp.einsum(
        "mhts,mshd->mthd", score_rounded, key_heads, preferred_element_type=jnp.float32
    ).astype(jnp.bfloat16)
    kv_grad = (
        jnp.stack([key_grad, value_grad], axis=2)
        .astype(jnp.bfloat16)
        .reshape(micro * sources, 2 * local_cols)
    )
    weight_grad = lax.dot_general(
        states_flat, kv_grad, (((0,), (0,)), ((), ())), preferred_element_type=jnp.float32
    )
    weight_grad = weight_grad.astype(jnp.bfloat16).reshape(1, model_width, 2, local_cols)
    kv_blocks = kv_grad.reshape(micro, sources, 2 * local_cols)
    full_term = jnp.einsum(
        "msk,dk->msd", kv_blocks, weight_flat, preferred_element_type=jnp.float32
    )
    feature_sum = lax.psum_scatter(
        full_term.astype(jnp.bfloat16), "mp", scatter_dimension=2, tiled=True
    )
    enc_grad = lax.psum_scatter(feature_sum, "section", scatter_dimension=0, tiled=True).astype(
        jnp.float32
    )
    return (
        context.reshape(1, micro, targets, local_cols),
        query_grad.reshape(1, micro, targets, local_cols),
        weight_grad,
        enc_grad.astype(jnp.bfloat16),
    )


def solution(mesh):
    return jax.shard_map(
        shards,
        mesh=mesh,
        in_specs=(
            P("section", None, "mp"),
            P(),
            P("section", None, None, "mp"),
            P("section", None, None, "mp"),
            P("section", None, None, "mp"),
        ),
        out_specs=(
            P("section", None, None, "mp"),
            P("section", None, None, "mp"),
            P("section", None, None, "mp"),
            P("section", None, "mp"),
        ),
        check_vma=False,
    )
```

profile of v0, /device:TPU:8, one launch (start us, length us, event | category | flops | bytes accessed | tf_op | source)
XLA Modules:
  0.0 354.8 jit_solution(9861248225377503961)
XLA Ops:
  7.2 31.0 %all_gather.6 = bf16[8,128,128]{2,1,0:T(8,128)(2,1)} all-gather(bf16[1,128,128]{2,1,0:T(8,128)(2,1)} %param.5), channel_id=1, replica_groups=mesh['section'=8,'mp'=32] {'section'}, dimensions={0}, use_global_device_ids=true | all-gather | bytes 294912 | tf_op jit(solution)/shard_map/all_gather | solution.py:16
  38.2 0.0 reduce-scatter.7.cloned.1.call-start
  38.3 2.3 copy.40
  40.6 2.3 copy.42
  42.8 3.2 reshape.77
  46.0 0.1 iota_compare_fusion
  46.1 78.9 %all-gather.2.cloned.1.call-done = bf16[8,128,4096]{2,1,0:T(8,128)(2,1)} async-done(((bf16[8,128,128]{2,1,0:T(8,128)(2,1)}), bf16[8,128,4096]{2,1,0:T(8,128)(2,1)}) %all-gather.2.cloned.1.call-update) | async-done | bytes 8388624 | tf_op jit(solution)/shard_map/all_gather | solution.py:17
  125.0 7.1 %fusion.19 = bf16[1024,256]{1,0:T(8,128)(2,1)} fusion(bf16[1024,4096]{1,0:T(8,128)(2,1)} %bitcast.130, bf16[512,8,2,128]{3,2,1,0:T(2,128)(2,1)} %bitcast.120), kind=kOutput, calls=%fused_computation.27 | convolution fusion | flops 2147745792 | bytes 11010048 | tf_op jit(solution)/shard_map/dot_general | solution.py:20
  132.1 2.5 reshape.81
  134.6 2.0 fusion.48
  136.6 1.9 copy.62
  138.5 1.4 copy.61
  139.9 3.9 %fusion.39 = f32[8,2,128,512]{3,2,1,0:T(8,128)} fusion(bf16[8,512,2,64]{1,3,2,0:T(8,128)(2,1)} %bitcast.118, bf16[8,128,1,2,64]{1,4,3,0,2:T(8,128)(2,1)S(1)} %copy.61), kind=kOutput, calls=%fused_computation.42 | convolution fusion | flops 134217728 | bytes 5505024 | tf_op jit(solution)/shard_map/mthd,mshd->mhts/dot_general | solution.py:46
  143.8 5.1 %fusion.49 = (f32[8,2,512]{2,1,0:T(2,128)S(1)}, f32[8,2,512,128]{2,3,1,0:T(8,128)}) fusion(pred[8,128]{1,0:T(8,128)(4,1)S(1)} %iota_compare_fusion, bf16[8,512,2,64]{1,3,2,0:T(8,128)(2,1)} %bitcast.123, bf16[8,128,1,2,64]{1,4,3,0,2:T(8,128)(2,1)} %copy.62), kind=kOutput, calls=%fused_computation.53 | convolution fusion | flops 138412160 | bytes 5538816 | tf_op jit(solution)/shard_map/sub | solution.py:37
  148.9 3.8 %fusion.24 = bf16[8,128,1,2,64]{1,4,3,0,2:T(8,128)(2,1)} fusion(bf16[8,512,2,64]{1,3,2,0:T(8,128)(2,1)S(1)} %bitcast.119, f32[8,2,512,128]{2,3,1,0:T(8,128)} %get-tuple-element.19, f32[8,2,512]{2,1,0:T(2,128)S(1)} %get-tuple-element.18), kind=kOutput, calls=%fused_computation.31 | convolution fusion | flops 136445952 | bytes 5537792 | tf_op jit(solution)/shard_map/mhts,mthd->mshd/dot_general | solution.py:43
  152.7 7.8 %fusion.23 = bf16[8,128,1,2,64]{1,4,3,0,2:T(8,128)(2,1)S(1)} fusion(bf16[8,512,2,64]{1,3,2,0:T(8,128)(2,1)} %bitcast.124, f32[8,2,128,512]{3,2,1,0:T(8,128)} %fusion.39, f32[8,2,512,128]{2,3,1,0:T(8,128)} %get-tuple-element.19, f32[8,2,512]{2,1,0:T(2,128)S(1)} %get-tuple-element.18), kind=kOutput, calls=%fused_computation.30 | convolution fusion | flops 141697152 | bytes 9732096 | tf_op jit(solution)/shard_map/mhts,mthd->mshd/dot_general | solution.py:51
  160.5 0.1 pad_maximum_fusion
  160.6 5.6 %convolution_convert_fusion = bf16[8,128,4096]{2,1,0:T(8,128)(2,1)} fusion(bf16[8,128,256]{1,2,0:T(8,128)(2,1)S(1)} %bitcast.122, bf16[4096,256,1]{1,0,2:T(8,128)(2,1)S(1)} %reshape.77), kind=kOutput, calls=%fused_computation.3 | convolution fusion | flops 2151677952 | bytes 11010048 | tf_op jit(solution)/shard_map/msk,dk->msd/dot_general | solution.py:67
  166.2 12.0 %copy.57 = bf16[8,128,4096]{1,0,2:T(8,128)(2,1)} copy(bf16[8,128,4096]{2,1,0:T(8,128)(2,1)} %convolution_convert_fusion) | data formatting | bytes 16777216
  178.2 8.8 %copy.78 = bf16[512,8,8,128]{3,1,2,0:T(8,128)(2,1)} copy(bf16[512,8,8,128]{3,2,1,0:T(8,128)(2,1)} %bitcast.117) | data formatting | bytes 16777216
  187.0 0.0 reduce-scatter.5.cloned.1.call-start
  187.1 0.3 copy.46
  187.4 2.7 convolution_convert_fusion.2
  190.1 1.5 copy.49
  191.7 7.6 %fusion.18 = bf16[8,2,64,512]{3,2,1,0:T(8,128)(2,1)S(1)} fusion(f32[8,2,128,512]{3,2,1,0:T(8,128)} %fusion.39, bf16[8,128,1,2,64]{1,4,3,0,2:T(8,128)(2,1)S(1)} %copy-done.1, f32[8,2,512,128]{2,3,1,0:T(8,128)} %get-tuple-element.19, f32[8,2,512]{2,1,0:T(2,128)S(1)} %get-tuple-element.18), kind=kOutput, calls=%fused_computation.26 | convolution fusion | flops 142090368 | bytes 9732096 | tf_op jit(solution)/shard_map/mhts,mshd->mthd/dot_general | solution.py:54
  199.2 1.3 copy.50
  200.6 105.5 %reduce-scatter.7.cloned.1.call-done = bf16[128,1024]{1,0:T(8,128)(2,1)} async-done(((bf16[4096,1024]{1,0:T(8,128)(2,1)}), bf16[128,1024]{1,0:T(8,128)(2,1)}) %reduce-scatter.7.cloned.1.call-update) | async-done | bytes 262160
  306.1 1.0 copy.66
  307.1 0.9 copy.58
  308.0 5.7 %convolution_convert_fusion.1 = bf16[256,4096]{1,0:T(8,128)(2,1)S(1)} fusion(bf16[1024,4096]{1,0:T(8,128)(2,1)} %bitcast.131, bf16[32,8,8,128]{3,2,1,0:T(8,128)(2,1)S(1)} %bitcast.128), kind=kOutput, calls=%fused_computation.4 | convolution fusion | flops 2148532224 | bytes 11010048 | tf_op jit(solution)/shard_map/dot_general | solution.py:62
  313.7 3.8 %copy.51 = bf16[1,4096,2,128]{3,2,1,0:T(2,128)(2,1)} copy(bf16[1,4096,2,128]{1,3,2,0:T(8,128)(2,1)S(1)} %bitcast.121) | data formatting | bytes 4194304
  317.5 30.8 %reduce-scatter.5.cloned.1.call-done = bf16[1,128,128]{2,1,0:T(8,128)(2,1)} async-done(((bf16[8,128,128]{2,1,0:T(8,128)(2,1)}), bf16[1,128,128]{2,1,0:T(8,128)(2,1)}) %reduce-scatter.5.cloned.1.call-update) | async-done | bytes 32784 | tf_op jit(solution)/shard_map/reduce_scatter | solution.py:73
  (13 shorter events, 0.1 us)
Async XLA Ops:
  7.2 117.8 %all-gather.2.cloned.1.call-start = ((), (), s32[]{:S(2)}) async-start(), calls=%async_computation.2 | async-start | bytes 8650752 | tf_op jit(solution)/shard_map/all_gather | solution.py:17
  38.2 7.8 %copy-start.3 = (s32[8]{0:T(128)S(1)}, s32[8]{0:T(128)}, u32[]{:S(2)}) copy-start(s32[8]{0:T(128)} %param.6) | copy-start | bytes 100
  38.2 267.8 %reduce-scatter.7.cloned.1.call-start = ((), (), s32[]{:S(2)}) async-start(), calls=%async_computation.4 | async-start | bytes 8650752
  143.8 5.1 %copy-start = (bf16[1,8,512,128]{2,3,1,0:T(8,128)(2,1)S(1)}, bf16[1,8,512,128]{2,3,1,0:T(8,128)(2,1)}, u32[]{:S(2)}) copy-start(bf16[1,8,512,128]{2,3,1,0:T(8,128)(2,1)} %copy.42) | copy-start | bytes 3145732
  152.7 7.8 %copy-start.2 = (bf16[8,128,1,2,64]{1,4,3,0,2:T(8,128)(2,1)S(1)}, bf16[8,128,1,2,64]{1,4,3,0,2:T(8,128)(2,1)}, u32[]{:S(2)}) copy-start(bf16[8,128,1,2,64]{1,4,3,0,2:T(8,128)(2,1)} %fusion.24) | copy-start | bytes 786436
  187.0 161.3 %reduce-scatter.5.cloned.1.call-start = ((), (), s32[]{:S(2)}) async-start(), calls=%async_computation.3 | async-start | bytes 294912 | tf_op jit(solution)/shard_map/reduce_scatter | solution.py:73
  187.4 4.2 %copy-start.1 = (bf16[8,128,1,2,64]{1,4,3,0,2:T(8,128)(2,1)S(1)}, bf16[8,128,1,2,64]{1,4,3,0,2:T(8,128)(2,1)}, u32[]{:S(2)}) copy-start(bf16[8,128,1,2,64]{1,4,3,0,2:T(8,128)(2,1)} %copy.62) | copy-start | bytes 786436
Sparse Core Ops, SparseCore 0:
  38.3 86.5 all-gather.1
  187.1 118.8 reduce-scatter.6
  309.2 39.1 reduce-scatter.4
where the time goes:
time: 356 us; the launch traced here: 355 us
  waiting for transfers between devices  215 us (60%)
  matrix products  49.3 us (14%)
  local copies, waits for them, and re-layouts  45.2 us (13%)
  blocking collectives  31 us (9%)
  between operations  13.9 us (4%)
    unnamed x4, waiting for transfers between devices  106 us
    all_gather x1, waiting for transfers between devices, shards(): states = lax.all_gather(across, 'mp', axis=2, tiled=True)  78.9 us
    unnamed x19, local copies, waits for them, and re-layouts  37.1 us
    all_gather x1, blocking collectives, shards(): across = lax.all_gather(enc_final, 'section', axis=0, tiled=True)  31 us
    reduce_scatter x1, waiting for transfers between devices, shards(): lax.psum_scatter(feature_sum, 'section', scatter_dimension=0, tiled=True)  30.8 us
    dot_general x1, matrix products, shards(): jnp.einsum('mhts,mthd->mshd', score_rounded, query_heads, preferred_eleme...  7.79 us
    dot_general x1, matrix products, shards(): jnp.einsum('mhts,mshd->mthd', score_rounded, key_heads, preferred_element...  7.59 us
  transfers between devices with their start and end apart: 3, of which 3 were waited for; matrix products, arithmetic and copies ran while one was open for 9% of the time, Pallas kernels for 0%

commit v1 on v0

--- a/solution.py
+++ b/solution.py
@@ -14,7 +14,9 @@
     targets = queries.shape[2]
     sources = enc_final.shape[1]
     across = lax.all_gather(enc_final, "section", axis=0, tiled=True)
-    states = lax.all_gather(across, "mp", axis=2, tiled=True)
+    states = jnp.concatenate(
+        lax.all_to_all(jnp.stack([across] * lax.axis_size("mp")), "mp", 0, 0), axis=2
+    )
     states_flat = states.reshape(micro * sources, model_width)
     weight_flat = kv_weight.reshape(model_width, 2 * local_cols)
     key_value = jnp.dot(states_flat, weight_flat, preferred_element_type=jnp.float32).astype(

time: 356 us -> 480 us (1.35)
  waiting for transfers between devices: 215 us -> 314 us
  local copies, waits for them, and re-layouts: 45.2 us -> 60.8 us
  starting transfers between devices: 0.12 us -> 12 us
    all_to_all x0 -> x1, waiting for transfers between devices: none -> 179 us  [shards(): lax.all_to_all(jnp.stack([across] * lax.axis_size('mp')), 'mp', 0, 0)]
    all_gather x1 -> x0, waiting for transfers between devices: 78.9 us -> none  [shards(): states = lax.all_gather(across, 'mp', axis=2, tiled=True)]
    reshape x0 -> x1, local copies, waits for them, and re-layouts: none -> 12.2 us  [shards(): jnp.concatenate(lax.all_to_all(jnp.stack([across] * lax.axis_size('mp')),...]
    all_to_all x0 -> x1, starting transfers between devices: none -> 12 us  [shards(): lax.all_to_all(jnp.stack([across] * lax.axis_size('mp')), 'mp', 0, 0)]
    another operation x0 -> x1, local copies, waits for them, and re-layouts: none -> 5.35 us  [shards(): jnp.stack([across] * lax.axis_size('mp'))]
    unnamed x19 -> x25, local copies, waits for them, and re-layouts: 37.1 us -> 35.2 us
    unnamed x4 -> x3, waiting for transfers between devices: 106 us -> 104 us
  transfers between devices with their start and end apart: 3 -> 3, of which waited for: 3 -> 3; matrix products, arithmetic and copies ran while one was open for 9% -> 6% of each run, Pallas kernels for 0% -> 0%
where the time goes in v1:
time: 480 us
  waiting for transfers between devices  314 us (65%)
  local copies, waits for them, and re-layouts  60.8 us (13%)
  matrix products  49.7 us (10%)
  blocking collectives  29.1 us (6%)
  between operations  14.2 us (3%)
  starting transfers between devices  12 us (2%)
    all_to_all x1, waiting for transfers between devices, shards(): lax.all_to_all(jnp.stack([across] * lax.axis_size('mp')), 'mp', 0, 0)  179 us
    unnamed x3, waiting for transfers between devices  104 us
    unnamed x25, local copies, waits for them, and re-layouts  35.2 us
    reduce_scatter x1, waiting for transfers between devices, shards(): lax.psum_scatter(feature_sum, 'section', scatter_dimension=0, tiled=True)  30.1 us
    all_gather x1, blocking collectives, shards(): across = lax.all_gather(enc_final, 'section', axis=0, tiled=True)  29.1 us
    reshape x1, local copies, waits for them, and re-layouts, shards(): jnp.concatenate(lax.all_to_all(jnp.stack([across] * lax.axis_size('mp')),...  12.2 us
    all_to_all x1, starting transfers between devices, shards(): lax.all_to_all(jnp.stack([across] * lax.axis_size('mp')), 'mp', 0, 0)  12 us
  transfers between devices with their start and end apart: 3, of which 3 were waited for; matrix products, arithmetic and copies ran while one was open for 6% of the time, Pallas kernels for 0%

profile of v1, /device:TPU:8, one launch (start us, length us, event | category | flops | bytes accessed | tf_op | source)
XLA Modules:
  0.0 479.6 jit_solution(15697676258237680492)
XLA Ops:
  7.2 29.1 %all_gather.3 = bf16[8,128,128]{2,1,0:T(8,128)(2,1)S(1)} all-gather(bf16[1,128,128]{2,1,0:T(8,128)(2,1)} %param.5), channel_id=1, replica_groups=mesh['section'=8,'mp'=32] {'section'}, dimensions={0}, use_global_device_ids=true | all-gather | bytes 294912 | tf_op jit(solution)/shard_map/all_gather | solution.py:16
  36.2 5.3 %stack.11 = bf16[32,8,128,128]{3,2,1,0:T(8,128)(2,1)} broadcast(bf16[8,128,128]{2,1,0:T(8,128)(2,1)S(1)} %all_gather.3), dimensions={1,2,3} | broadcast | bytes 8650752 | tf_op jit(solution)/shard_map/stack | solution.py:18
  41.6 12.0 %all-to-all-start = ((bf16[32,8,128,128]{3,2,1,0:T(8,128)(2,1)}), bf16[32,8,128,128]{3,2,1,0:T(8,128)(2,1)}, u32[]{:S(2)}, u32[]{:S(2)}) async-start(bf16[32,8,128,128]{3,2,1,0:T(8,128)(2,1)} %stack.11), calls=%async_computation | async-start | bytes 16777216 | tf_op jit(solution)/shard_map/all_to_all | solution.py:18
  53.6 1.3 copy.41
  55.0 1.3 copy.43
  56.3 3.2 reshape.79
  59.4 0.1 iota_compare_fusion
  59.5 179.3 %all-to-all-done = bf16[32,8,128,128]{3,2,1,0:T(8,128)(2,1)} async-done(((bf16[32,8,128,128]{3,2,1,0:T(8,128)(2,1)}), bf16[32,8,128,128]{3,2,1,0:T(8,128)(2,1)}, u32[]{:S(2)}, u32[]{:S(2)}) %all-to-all-start) | async-done | bytes 8388640 | tf_op jit(solution)/shard_map/all_to_all | solution.py:18
  238.8 12.2 %copy.37 = bf16[8,128,32,128]{3,2,1,0:T(8,128)(2,1)} copy(bf16[8,128,32,128]{3,1,0,2:T(8,128)(2,1)} %bitcast) | data formatting | bytes 16777216 | tf_op jit(solution)/shard_map/reshape | solution.py:17
  251.0 6.7 %fusion.27 = bf16[1024,256]{1,0:T(8,128)(2,1)} fusion(bf16[512,8,2,128]{3,2,1,0:T(2,128)(2,1)S(1)} %bitcast.131, bf16[128,8,32,128]{3,2,1,0:T(8,128)(2,1)} %bitcast.127), kind=kOutput, calls=%fused_computation.32 | convolution fusion | flops 2147745792 | bytes 11010048 | tf_op jit(solution)/shard_map/dot_general | solution.py:22
  257.6 2.5 reshape.83
  260.1 2.0 fusion.58
  262.1 1.9 copy.63
  264.0 1.4 copy.62
  265.4 3.9 fusion.49
  269.4 5.1 %fusion.59 = (f32[8,2,512]{2,1,0:T(2,128)S(1)}, f32[8,2,512,128]{2,3,1,0:T(8,128)}) fusion(pred[8,128]{1,0:T(8,128)(4,1)S(1)} %iota_compare_fusion, bf16[8,512,2,64]{1,3,2,0:T(8,128)(2,1)} %bitcast.134, bf16[8,128,1,2,64]{1,4,3,0,2:T(8,128)(2,1)} %copy.63), kind=kOutput, calls=%fused_computation.58 | convolution fusion | flops 138412160 | bytes 5538816 | tf_op jit(solution)/shard_map/sub | solution.py:39
  274.5 3.8 fusion.34
  278.2 7.8 %fusion.33 = bf16[8,128,1,2,64]{1,4,3,0,2:T(8,128)(2,1)S(1)} fusion(bf16[8,512,2,64]{1,3,2,0:T(8,128)(2,1)} %bitcast.135, f32[8,2,128,512]{3,2,1,0:T(8,128)} %fusion.49, f32[8,2,512,128]{2,3,1,0:T(8,128)} %get-tuple-element.19, f32[8,2,512]{2,1,0:T(2,128)S(1)} %get-tuple-element.18), kind=kOutput, calls=%fused_computation.35 | convolution fusion | flops 141697152 | bytes 9732096 | tf_op jit(solution)/shard_map/mhts,mthd->mshd/dot_general | solution.py:53
  286.1 5.6 %convolution_convert_fusion = bf16[8,128,4096]{2,1,0:T(8,128)(2,1)} fusion(bf16[8,128,256]{1,2,0:T(8,128)(2,1)S(1)} %bitcast.133, bf16[4096,256,1]{1,0,2:T(8,128)(2,1)S(1)} %reshape.79), kind=kOutput, calls=%fused_computation.7 | convolution fusion | flops 2151677952 | bytes 11010048 | tf_op jit(solution)/shard_map/msk,dk->msd/dot_general | solution.py:69
  291.7 12.0 %copy.58 = bf16[8,128,4096]{1,0,2:T(8,128)(2,1)} copy(bf16[8,128,4096]{2,1,0:T(8,128)(2,1)} %convolution_convert_fusion) | data formatting | bytes 16777216
  303.8 8.8 %copy.92 = bf16[512,8,8,128]{3,1,2,0:T(8,128)(2,1)} copy(bf16[512,8,8,128]{3,2,1,0:T(8,128)(2,1)} %bitcast.126) | data formatting | bytes 16777216
  312.6 0.3 copy.47
  313.0 2.7 convolution_convert_fusion.1
  315.7 1.5 copy.50
  317.2 7.8 %fusion.26 = bf16[8,2,64,512]{3,2,1,0:T(8,128)(2,1)S(1)} fusion(f32[8,2,128,512]{3,2,1,0:T(8,128)} %fusion.49, bf16[8,128,1,2,64]{1,4,3,0,2:T(8,128)(2,1)S(1)} %copy-done.4, f32[8,2,512,128]{2,3,1,0:T(8,128)} %get-tuple-element.19, f32[8,2,512]{2,1,0:T(2,128)S(1)} %get-tuple-element.18), kind=kOutput, calls=%fused_computation.31 | convolution fusion | flops 142090368 | bytes 9732096 | tf_op jit(solution)/shard_map/mhts,mshd->mthd/dot_general | solution.py:56
  325.0 1.3 copy.51
  326.3 104.2 %reduce-scatter.7.cloned.1.call-done = bf16[128,1024]{1,0:T(8,128)(2,1)} async-done(((bf16[4096,1024]{1,0:T(8,128)(2,1)}), bf16[128,1024]{1,0:T(8,128)(2,1)}) %reduce-scatter.7.cloned.1.call-update) | async-done | bytes 262160
  430.5 1.0 copy.68
  431.5 0.9 copy.59
  432.5 6.4 %fusion.8 = bf16[256,4096]{1,0:T(8,128)(2,1)S(1)} fusion(bf16[128,8,32,128]{3,2,1,0:T(8,128)(2,1)} %bitcast.128, bf16[32,8,8,128]{3,2,1,0:T(8,128)(2,1)S(1)} %bitcast.139), kind=kOutput, calls=%fused_computation.10 | convolution fusion | flops 2148532224 | bytes 11010048 | tf_op jit(solution)/shard_map/dot_general | solution.py:64
  438.8 3.8 copy.52
  442.6 30.1 %reduce-scatter.5.cloned.1.call-done = bf16[1,128,128]{2,1,0:T(8,128)(2,1)} async-done(((bf16[8,128,128]{2,1,0:T(8,128)(2,1)}), bf16[1,128,128]{2,1,0:T(8,128)(2,1)}) %reduce-scatter.5.cloned.1.call-update) | async-done | bytes 32784 | tf_op jit(solution)/shard_map/reduce_scatter | solution.py:75
  (20 shorter events, 0.2 us)
Async XLA Ops:
  41.6 12.0 %copy-start.2 = (bf16[1,8,512,128]{3,2,1,0:T(8,128)(2,1)S(1)}, bf16[1,8,512,128]{3,2,1,0:T(8,128)(2,1)}, u32[]{:S(2)}) copy-start(bf16[1,8,512,128]{3,2,1,0:T(8,128)(2,1)} %param.8) | copy-start | bytes 3145732
  41.6 13.4 %copy-start.3 = (bf16[1,8,512,128]{3,2,1,0:T(8,128)(2,1)S(1)}, bf16[1,8,512,128]{3,2,1,0:T(8,128)(2,1)}, u32[]{:S(2)}) copy-start(bf16[1,8,512,128]{3,2,1,0:T(8,128)(2,1)} %param.9) | copy-start | bytes 3145732
  41.6 197.2 %all-to-all-start = ((bf16[32,8,128,128]{3,2,1,0:T(8,128)(2,1)}), bf16[32,8,128,128]{3,2,1,0:T(8,128)(2,1)}, u32[]{:S(2)}, u32[]{:S(2)}) async-start(bf16[32,8,128,128]{3,2,1,0:T(8,128)(2,1)} %stack.11), calls=%async_computation | async-start | bytes 16777216 | tf_op jit(solution)/shard_map/all_to_all | solution.py:18
  53.6 5.9 %copy-start.6 = (s32[8]{0:T(128)S(1)}, s32[8]{0:T(128)}, u32[]{:S(2)}) copy-start(s32[8]{0:T(128)} %param.6) | copy-start | bytes 100
  53.6 377.0 %reduce-scatter.7.cloned.1.call-start = ((), (), s32[]{:S(2)}) async-start(), calls=%async_computation.4 | async-start | bytes 8650752
  238.8 12.2 %copy-start.1 = (bf16[1,4096,2,128]{3,2,1,0:T(2,128)(2,1)S(1)}, bf16[1,4096,2,128]{3,2,1,0:T(2,128)(2,1)}, u32[]{:S(2)}) copy-start(bf16[1,4096,2,128]{3,2,1,0:T(2,128)(2,1)} %param.7) | copy-start | bytes 6291460
  269.4 5.1 %copy-start = (bf16[1,8,512,128]{2,3,1,0:T(8,128)(2,1)S(1)}, bf16[1,8,512,128]{2,3,1,0:T(8,128)(2,1)}, u32[]{:S(2)}) copy-start(bf16[1,8,512,128]{2,3,1,0:T(8,128)(2,1)} %copy.43) | copy-start | bytes 3145732
  278.2 7.8 %copy-start.5 = (bf16[8,128,1,2,64]{1,4,3,0,2:T(8,128)(2,1)S(1)}, bf16[8,128,1,2,64]{1,4,3,0,2:T(8,128)(2,1)}, u32[]{:S(2)}) copy-start(bf16[8,128,1,2,64]{1,4,3,0,2:T(8,128)(2,1)} %fusion.34) | copy-start | bytes 786436
  312.6 160.2 %reduce-scatter.5.cloned.1.call-start = ((), (), s32[]{:S(2)}) async-start(), calls=%async_computation.3 | async-start | bytes 294912 | tf_op jit(solution)/shard_map/reduce_scatter | solution.py:75
  313.0 4.2 copy-start.4
Sparse Core Ops, SparseCore 0:
  312.7 117.8 reduce-scatter.6
  433.6 39.0 reduce-scatter.4
